TPU v7x, 256 devices: a whole 4x4x8 slice. The times are simulated.
256 devices in a mesh: wide: 64 (over x, z, y_hi), narrow: 4 (over y_lo, core).
Axes of the slice: x: 4, y: 4 (y_hi: 2, y_lo: 2; y = y_hi * 2 + y_lo), z: 8, core: 2. Of those that a mesh axis runs over, the one named last changes fastest.
Arguments:
- latent: bfloat16 [64, 32, 48, 256], P('wide', 'narrow'), may hold values from -12 to 12
- conv_first: bfloat16 [6912, 256], P(None, 'wide'), may hold values from -0.078125 to 0.078125
- conv_second: bfloat16 [6912, 256], P(None, 'wide'), may hold values from -0.078125 to 0.078125
- embed_weight: bfloat16 [1024, 2240], P(None, 'wide'), may hold values from -0.1875 to 0.1875
- qkv_weight: bfloat16 [3, 2240, 2240], P(None, None, 'narrow'), may hold values from -0.125 to 0.125
Outputs:
- mixed: bfloat16 [24576, 2240], P('wide', 'narrow')
All inputs are finite; a program needn't handle non-finite values.
Results may differ from a plain program's by a relative error of at most 0.011.
Values may be sent and summed in bfloat16 or wider, within the bound.
No kernel may reach another device: no remote copies, remote signals or barrier semaphores. Data moves between devices by JAX's collectives and lax.ppermute only.
A program may use at most 128 MiB of HBM per device.

v0:
```python
import jax
import jax.numpy as jnp
from jax import lax
from jax.sharding import PartitionSpec as P

HEAD_DIM = 112


def shifted(x, axis, by):
    size = lax.axis_size(axis)
    pairs = [(i, i + by) for i in range(size) if 0 <= i + by < size]
    return lax.ppermute(x, axis, pairs)


def extended(block, sides, width):
    for axis, dim in sides:
        count = lax.axis_size(axis)
        forward = [(i, i + 1) for i in range(count - 1)]
        backward = [(target, source) for source, target in forward]
        low = lax.ppermute(
            lax.slice_in_dim(block, block.shape[dim] - width, None, axis=dim), axis, forward
        )
        high = lax.ppermute(lax.slice_in_dim(block, 0, width, axis=dim), axis, backward)
        block = jnp.concatenate([low, block, high], axis=dim)
    return block


def laid_out(blocks, dim):
    lengths = list(blocks.shape[1:])
    lengths[dim] *= blocks.shape[0]
    return jnp.moveaxis(blocks, 0, dim).reshape(lengths)


def work_in_pieces(x, axis, dim, work, out_dim):
    extent = x.shape[dim]
    pieces = jnp.split(x, 2, axis=dim) if extent % 2 == 0 else [x]
    first = jnp.arange(lax.axis_size(axis)) * extent
    blocks = [lax.all_gather(share, axis) for share in pieces]
    made = [jax.vmap(work)(b, first + k * (extent // len(pieces))) for k, b in enumerate(blocks)]
    return laid_out(jnp.concatenate(made, axis=out_dim + 1), out_dim)


def exchange_in_groups(x, axis, split_dim, concat_dim, work, item_dim, out_dim):

    def moved(group):
        return lax.all_to_all(group, axis, split_axis=split_dim, concat_axis=concat_dim, tiled=True)

    items = jax.tree.leaves(x)[0].shape[item_dim]
    ends = [items * k // 2 for k in range(2 + 1)] if items % 2 == 0 else [0, items]
    groups = [
        jax.tree.map(lambda a: lax.slice_in_dim(a, low, high, axis=item_dim), x)
        for low, high in zip(ends, ends[1:])
    ]
    arrived = [moved(group) for group in groups]
    made = [work(group) for group in arrived]
    return jax.tree.map(lambda *parts: jnp.concatenate(parts, axis=out_dim), *made)


def causal_conv(current, weight):
    before = shifted(current, "wide", 1)
    earlier = shifted(current, "wide", 2)
    stacked = jnp.concatenate([earlier, before, current], axis=0)
    rimmed = extended(stacked, (("narrow", 1),), 1)
    padded = jnp.pad(rimmed, ((0, 0), (0, 0), (1, 1), (0, 0)))
    row_count = current.shape[1]
    col_count = current.shape[2]
    chan_count = current.shape[3]
    block_cols = lax.all_gather(weight, "wide", axis=1, tiled=True)
    summed = jnp.zeros((row_count * col_count, block_cols.shape[1]), jnp.float32)
    for kernel_tap in range(27):
        time_step = kernel_tap // 9
        row_step = kernel_tap // 3 % 3
        col_step = kernel_tap % 3
        window = padded[time_step, row_step : row_step + row_count, col_step : col_step + col_count]
        window = window.reshape(row_count * col_count, chan_count)
        summed = summed + jnp.dot(
            window,
            block_cols[kernel_tap * chan_count : (kernel_tap + 1) * chan_count],
            preferred_element_type=jnp.float32,
        )
    return summed


def embed_tokens(patch_feats, embed_weight):

    def project(block_cols, offset):
        return jnp.dot(patch_feats, block_cols, preferred_element_type=jnp.float32)

    return work_in_pieces(embed_weight, "wide", 1, project, 1).astype(jnp.bfloat16)


def per_device(latent, conv_first, conv_second, embed_weight, qkv_weight):
    row_count = latent.shape[1]
    col_count = latent.shape[2]
    chan_count = latent.shape[3]
    first = causal_conv(latent, conv_first)
    activated = jax.nn.silu(first).astype(jnp.bfloat16).reshape(latent.shape)
    second = causal_conv(activated, conv_second) + latent.reshape(-1, chan_count).astype(
        jnp.float32
    )
    block_out = second.astype(jnp.bfloat16)
    patches = block_out.reshape(row_count // 2, 2, col_count // 2, 2, chan_count)
    patches = patches.transpose(0, 2, 1, 3, 4).reshape(-1, 4 * chan_count)
    whole_patches = lax.all_gather(patches, "narrow", axis=0, tiled=True)
    embedded = embed_tokens(whole_patches, embed_weight)
    heads_here = qkv_weight.shape[2] // HEAD_DIM
    token_count = embedded.shape[0]
    query_raw = jnp.dot(embedded, qkv_weight[0], preferred_element_type=jnp.float32)
    key_raw = jnp.dot(embedded, qkv_weight[1], preferred_element_type=jnp.float32)
    val_rows = jnp.dot(embedded, qkv_weight[2], preferred_element_type=jnp.float32).astype(
        jnp.bfloat16
    )
    query_feat = (
        (jax.nn.elu(query_raw) + 1.0)
        .astype(jnp.bfloat16)
        .reshape(token_count, heads_here, HEAD_DIM)
    )
    key_feat = (
        (jax.nn.elu(key_raw) + 1.0).astype(jnp.bfloat16).reshape(token_count, heads_here, HEAD_DIM)
    )
    val_heads = val_rows.reshape(token_count, heads_here, HEAD_DIM)
    scores = jnp.einsum("thd,shd->hts", query_feat, key_feat, preferred_element_type=jnp.float32)
    row_ids = lax.broadcasted_iota(jnp.int32, (token_count, token_count), 0)
    col_ids = lax.broadcasted_iota(jnp.int32, (token_count, token_count), 1)
    scores = jnp.where((col_ids <= row_ids)[None], scores, 0.0)
    local_den = jnp.sum(scores, axis=-1)
    local_num = jnp.einsum(
        "hts,she->the", scores.astype(jnp.bfloat16), val_heads, preferred_element_type=jnp.float32
    )
    state_local = jnp.einsum(
        "thd,the->hde", key_feat, val_heads, preferred_element_type=jnp.float32
    )
    key_local = jnp.sum(key_feat, axis=0, dtype=jnp.float32)
    flat_state = jnp.concatenate([state_local.reshape(-1), key_local.reshape(-1)])
    length_all = flat_state.shape[0]
    peer_count = lax.axis_size("wide")
    per_peer = -(-length_all // peer_count)
    piece_grid = jnp.pad(flat_state, (0, per_peer * peer_count - length_all)).reshape(
        peer_count, per_peer
    )
    lower_ones = (
        lax.broadcasted_iota(jnp.int32, (peer_count, peer_count), 1)
        < lax.broadcasted_iota(jnp.int32, (peer_count, peer_count), 0)
    ).astype(jnp.float32)

    def running(columns_in):
        partial_sums = jnp.dot(lower_ones, columns_in, precision=lax.Precision.HIGHEST)
        return lax.all_to_all(
            partial_sums.astype(jnp.bfloat16), "wide", split_axis=0, concat_axis=0, tiled=True
        ).astype(partial_sums.dtype)

    spread = exchange_in_groups(
        piece_grid.astype(jnp.bfloat16),
        "wide",
        0,
        0,
        lambda group: running(group.astype(jnp.float32)),
        1,
        1,
    )
    flat_prefix = spread.reshape(-1)[:length_all]
    state_size = state_local.size
    state_prev = flat_prefix[:state_size].reshape(state_local.shape)
    key_prev = flat_prefix[state_size:].reshape(key_local.shape)
    query_wide = query_feat.astype(jnp.float32)
    carried_num = jnp.einsum(
        "thd,hde->the", query_wide, state_prev, precision=lax.Precision.HIGHEST
    )
    carried_den = jnp.einsum("thd,hd->th", query_wide, key_prev, precision=lax.Precision.HIGHEST)
    result = (local_num + carried_num) / (local_den.T + carried_den)[..., None]
    return result.astype(jnp.bfloat16).reshape(token_count, heads_here * HEAD_DIM)


def solution(mesh):
    return jax.shard_map(
        per_device,
        mesh=mesh,
        in_specs=(
            P("wide", "narrow", None, None),
            P(None, "wide"),
            P(None, "wide"),
            P(None, "wide"),
            P(None, None, "narrow"),
        ),
        out_specs=P("wide", "narrow"),
        check_vma=False,
    )
```

profile of v0, /device:TPU:8, one launch (start us, length us, event | category | flops | bytes accessed | tf_op | source)
XLA Modules:
  0.0 465.5 jit_solution(17870810909222242809)
XLA Ops:
  6.5 0.7 all-gather.9.cloned.1.call-update
  7.3 0.7 all-gather.11.cloned.1.call-update
  8.1 3.8 collective-permute-start
  11.9 4.2 collective-permute-start.1
  16.4 3.9 collective-permute-done.1
  20.3 1.0 constant_dynamic-update-slice_fusion
  21.4 1.9 collective-permute-start.2
  23.3 3.6 collective-permute-start.3
  27.0 1.9 collective-permute-done.3
  29.0 0.4 fusion.68
  29.4 1.8 fusion.150
  31.2 1.1 pad_maximum_fusion.10
  32.3 105.1 %all-gather.9.cloned.1.call-done = bf16[64,4,6912]{2,1,0:T(4,128)(2,1)} async-done(((bf16[1,4,6912]{2,1,0:T(4,128)(2,1)}), bf16[64,4,6912]{2,1,0:T(4,128)(2,1)}) %all-gather.9.cloned.1.call-update) | async-done | bytes 3538960 | tf_op jit(solution)/shard_map/all_gather | solution.py:68
  137.5 5.3 %reshape.81 = bf16[256,6912]{1,0:T(8,128)(2,1)S(1)} reshape(bf16[64,4,6912]{2,1,0:T(4,128)(2,1)} %all-gather.9.cloned.1.call-done) | data formatting | bytes 7077888
  142.8 1.2 fusion.142
  144.1 1.2 fusion.136
  145.2 1.2 fusion.132
  146.4 1.2 fusion.128
  147.6 1.2 fusion.124
  150.7 0.2 fusion.27
  151.8 0.2 fusion.29
  152.3 0.2 fusion.30
  154.4 0.3 multiply_convert_fusion
  154.7 2.8 collective-permute-start.4
  157.6 3.3 collective-permute-start.5
  160.9 3.1 collective-permute-done.5
  164.1 0.7 pad_maximum_fusion.18
  164.8 1.9 collective-permute-start.7
  166.7 0.7 iota_compare_fusion.2
  167.4 94.9 %all-gather.11.cloned.1.call-done = bf16[64,4,6912]{2,1,0:T(4,128)(2,1)} async-done(((bf16[1,4,6912]{2,1,0:T(4,128)(2,1)}), bf16[64,4,6912]{2,1,0:T(4,128)(2,1)}) %all-gather.11.cloned.1.call-update) | async-done | bytes 3538960 | tf_op jit(solution)/shard_map/all_gather | solution.py:68
  262.3 5.3 %reshape.83 = bf16[256,6912]{1,0:T(8,128)(2,1)S(1)} reshape(bf16[64,4,6912]{2,1,0:T(4,128)(2,1)} %all-gather.11.cloned.1.call-done) | data formatting | bytes 7077888
  267.6 1.9 collective-permute-start.6
  269.6 1.2 pad_maximum_fusion
  270.8 2.7 collective-permute-done.6
  273.5 1.2 pad_maximum_fusion.3
  274.7 1.6 select_maximum_fusion
  276.3 0.5 fusion.149
  280.1 0.3 fusion.34
  280.6 0.2 fusion.35
  281.1 0.2 fusion.36
  281.6 0.2 fusion.37
  283.4 0.9 fusion.41
  284.3 1.0 reshape.69
  285.6 7.4 %all_gather.17 = bf16[384,1024]{1,0:T(8,128)(2,1)S(1)} all-gather(bf16[96,1024]{1,0:T(8,128)(2,1)S(1)} %reshape.70), channel_id=1, replica_groups=mesh['wide'=64,'narrow'=4] {'narrow'}, dimensions={0}, use_global_device_ids=true | all-gather | bytes 983040 | tf_op jit(solution)/shard_map/all_gather | solution.py:104
  293.0 101.8 %all-gather.7.cloned.1.call-done = bf16[65536,35]{0,1:T(8,128)(2,1)} async-done(((bf16[1024,35]{0,1:T(8,128)(2,1)}), bf16[65536,35]{0,1:T(8,128)(2,1)}) %all-gather.7.cloned.1.call-update) | async-done | bytes 4587536 | tf_op jit(solution)/shard_map/all_gather | solution.py:38
  394.7 5.5 %copy.29 = bf16[5,8,64,1024]{3,2,1,0:T(8,128)(2,1)S(1)} copy(bf16[5,8,64,1024]{3,1,2,0:T(8,128)(2,1)} %bitcast.244) | data formatting | bytes 10485760
  400.2 2.6 fusion.12
  402.8 1.0 copy.19
  403.8 1.5 convert_element_type.63
  405.4 4.2 fusion.152
  409.6 3.2 fusion.22
  412.8 0.3 convolution_convert_fusion
  413.1 0.3 reshape.74
  413.4 0.9 convert_element_type.72
  414.4 8.1 %all-to-all-start = ((bf16[64,1,989]{2,1,0:T(2,128)(2,1)}), bf16[64,1,989]{2,1,0:T(2,128)(2,1)S(1)}, u32[]{:S(2)}, u32[]{:S(2)}) async-start(bf16[64,1,989]{2,1,0:T(2,128)(2,1)} %convert_element_type.72), calls=%async_computation | async-start | bytes 524288 | tf_op jit(solution)/shard_map/all_to_all | solution.py:46
  422.5 3.5 fusion.49
  425.9 9.1 %all-to-all-done = bf16[64,1,989]{2,1,0:T(2,128)(2,1)S(1)} async-done(((bf16[64,1,989]{2,1,0:T(2,128)(2,1)}), bf16[64,1,989]{2,1,0:T(2,128)(2,1)S(1)}, u32[]{:S(2)}, u32[]{:S(2)}) %all-to-all-start) | async-done | bytes 126624 | tf_op jit(solution)/shard_map/all_to_all | solution.py:46
  435.2 0.9 copy.22
  436.1 5.8 %all-to-all-start.1 = ((bf16[64,1,989]{2,1,0:T(2,128)(2,1)}), bf16[64,1,989]{2,1,0:T(2,128)(2,1)S(1)}, u32[]{:S(2)}, u32[]{:S(2)}) async-start(bf16[64,1,989]{2,1,0:T(2,128)(2,1)} %copy.22), calls=%async_computation.1 | async-start | bytes 524288 | tf_op jit(solution)/shard_map/all_to_all | solution.py:148
  441.9 1.8 select_reduce_fusion
  443.8 10.7 %all-to-all-done.1 = bf16[64,1,989]{2,1,0:T(2,128)(2,1)S(1)} async-done(((bf16[64,1,989]{2,1,0:T(2,128)(2,1)}), bf16[64,1,989]{2,1,0:T(2,128)(2,1)S(1)}, u32[]{:S(2)}, u32[]{:S(2)}) %all-to-all-start.1) | async-done | bytes 126624 | tf_op jit(solution)/shard_map/all_to_all | solution.py:148
  454.5 0.8 reduce.2
  456.0 0.3 fusion.153
  456.3 2.6 fusion.25
  (127 shorter events, 11.4 us)
Async XLA Ops:
  6.5 130.9 %all-gather.9.cloned.1.call-start = ((), (), s32[]{:S(2)}) async-start(), calls=%async_computation.3 | async-start | bytes 3594240 | tf_op jit(solution)/shard_map/all_gather | solution.py:68
  7.3 255.1 %all-gather.11.cloned.1.call-start = ((), (), s32[]{:S(2)}) async-start(), calls=%async_computation.4 | async-start | bytes 3594240 | tf_op jit(solution)/shard_map/all_gather | solution.py:68
  8.0 386.7 %all-gather.7.cloned.1.call-start = ((), (), s32[]{:S(2)}) async-start(), calls=%async_computation.2 | async-start | bytes 5324800 | tf_op jit(solution)/shard_map/all_gather | solution.py:38
  8.1 8.3 %collective-permute-start = (bf16[1,8,48,256]{3,2,1,0:T(8,128)(2,1)}, bf16[1,8,48,256]{3,2,1,0:T(8,128)(2,1)S(1)}, u32[]{:S(2)}, u32[]{:S(2)}) collective-permute-start(bf16[1,8,48,256]{3,2,1,0:T(8,128)(2,1)} %param.5), channel_id=1, source_target_pairs={{0,8},{4,12},{8,16},{12,20},{16,24},{20,28},{24,32},{28,36},{32,40... | collective-permute-start | bytes 589832 | tf_op jit(solution)/shard_map/ppermute | solution.py:12
  11.9 8.4 %collective-permute-start.1 = (bf16[1,8,48,256]{3,2,1,0:T(8,128)(2,1)}, bf16[1,8,48,256]{3,2,1,0:T(8,128)(2,1)S(1)}, u32[]{:S(2)}, u32[]{:S(2)}) collective-permute-start(bf16[1,8,48,256]{3,2,1,0:T(8,128)(2,1)} %param.5), channel_id=1, source_target_pairs={{0,4},{4,8},{8,12},{12,16},{16,20},{20,24},{24,28},{28,32},{32,36}... | collective-permute-start | bytes 589832 | tf_op jit(solution)/shard_map/ppermute | solution.py:12
  16.3 5.0 %copy-start.29 = (bf16[1,8,48,256]{3,2,1,0:T(8,128)(2,1)}, bf16[1,8,48,256]{3,2,1,0:T(8,128)(2,1)S(1)}, u32[]{:S(2)}) copy-start(bf16[1,8,48,256]{3,2,1,0:T(8,128)(2,1)S(1)} %collective-permute-done) | copy-start | bytes 589828
  20.3 1.0 copy-start.27
  21.4 5.7 %collective-permute-start.2 = (bf16[3,1,48,256]{3,2,1,0:T(8,128)(2,1)S(1)}, bf16[3,1,48,256]{3,2,1,0:T(8,128)(2,1)S(1)}, u32[]{:S(2)}, u32[]{:S(2)}) collective-permute-start(bf16[3,1,48,256]{3,2,1,0:T(8,128)(2,1)S(1)} %get-tuple-element.58), channel_id=1, source_target_pairs={{0,1},{1,2},{2,3},{4,5},{5,6},{6,7},{8,9},{9,10},{10,11},{12,13},{... | collective-permute-start | bytes 221192 | tf_op jit(solution)/shard_map/ppermute | solution.py:20
  23.3 5.7 %collective-permute-start.3 = (bf16[3,1,48,256]{3,2,1,0:T(8,128)(2,1)S(1)}, bf16[3,1,48,256]{3,2,1,0:T(8,128)(2,1)S(1)}, u32[]{:S(2)}, u32[]{:S(2)}) collective-permute-start(bf16[3,1,48,256]{3,2,1,0:T(8,128)(2,1)S(1)} %get-tuple-element.59), channel_id=1, source_target_pairs={{1,0},{2,1},{3,2},{5,4},{6,5},{7,6},{9,8},{10,9},{11,10},{13,12},{... | collective-permute-start | bytes 221192 | tf_op jit(solution)/shard_map/ppermute | solution.py:23
  142.8 6.1 %copy-start.11 = (bf16[1,8,48,256]{3,2,1,0:T(8,128)(2,1)S(1)}, bf16[1,8,48,256]{3,2,1,0:T(8,128)(2,1)}, u32[]{:S(2)}) copy-start(bf16[1,8,48,256]{3,2,1,0:T(8,128)(2,1)} %get-tuple-element.28) | copy-start | bytes 589828
  142.8 6.3 %copy-start.10 = (bf16[1,8,48,256]{3,2,1,0:T(8,128)(2,1)S(1)}, bf16[1,8,48,256]{3,2,1,0:T(8,128)(2,1)}, u32[]{:S(2)}) copy-start(bf16[1,8,48,256]{3,2,1,0:T(8,128)(2,1)} %get-tuple-element.26) | copy-start | bytes 589828
  142.8 6.6 %copy-start.26 = (bf16[1,8,48,256]{3,2,1,0:T(8,128)(2,1)S(1)}, bf16[1,8,48,256]{3,2,1,0:T(8,128)(2,1)}, u32[]{:S(2)}) copy-start(bf16[1,8,48,256]{3,2,1,0:T(8,128)(2,1)} %get-tuple-element.55) | copy-start | bytes 589828
  142.8 6.8 %copy-start.21 = (bf16[1,8,48,256]{3,2,1,0:T(8,128)(2,1)S(1)}, bf16[1,8,48,256]{3,2,1,0:T(8,128)(2,1)}, u32[]{:S(2)}) copy-start(bf16[1,8,48,256]{3,2,1,0:T(8,128)(2,1)} %get-tuple-element.38) | copy-start | bytes 589828
  142.8 7.1 %copy-start.20 = (bf16[1,8,48,256]{3,2,1,0:T(8,128)(2,1)S(1)}, bf16[1,8,48,256]{3,2,1,0:T(8,128)(2,1)}, u32[]{:S(2)}) copy-start(bf16[1,8,48,256]{3,2,1,0:T(8,128)(2,1)} %get-tuple-element.37) | copy-start | bytes 589828
  145.2 4.9 %copy-start.30 = (bf16[1,8,48,256]{3,2,1,0:T(8,128)(2,1)S(1)}, bf16[1,8,48,256]{3,2,1,0:T(8,128)(2,1)}, u32[]{:S(2)}) copy-start(bf16[1,8,48,256]{3,2,1,0:T(8,128)(2,1)} %copy-done.29) | copy-start | bytes 589828
  147.6 2.8 copy-start.19
  148.8 1.8 copy-start.25
  149.3 1.6 copy-start.18
  149.6 1.6 copy-start.24
  150.1 1.4 copy-start.17
  150.4 1.4 copy-start.28
  150.7 1.4 copy-start.16
  150.9 1.4 copy-start.23
  151.2 1.4 copy-start.15
  151.5 1.4 copy-start.22
  151.7 1.4 copy-start.14
  152.0 1.4 copy-start.6
  152.0 1.6 copy-start.13
  152.3 1.6 copy-start.9
  152.6 1.6 copy-start.12
  152.8 1.6 copy-start.31
  154.7 9.4 %copy-start = (bf16[384,256]{1,0:T(8,128)(2,1)}, bf16[384,256]{1,0:T(8,128)(2,1)S(1)}, u32[]{:S(2)}) copy-start(bf16[384,256]{1,0:T(8,128)(2,1)S(1)} %multiply_convert_fusion) | copy-start | bytes 589828
  154.7 6.2 %collective-permute-start.4 = (bf16[1,8,48,256]{3,2,1,0:T(8,128)(2,1)S(1)}, bf16[1,8,48,256]{3,2,1,0:T(8,128)(2,1)S(1)}, u32[]{:S(2)}, u32[]{:S(2)}) collective-permute-start(bf16[1,8,48,256]{3,2,1,0:T(8,128)(2,1)S(1)} %bitcast.246), channel_id=1, source_target_pairs={{0,8},{4,12},{8,16},{12,20},{16,24},{20,28},{24,32},{28,36},{32,40... | collective-permute-start | bytes 589832 | tf_op jit(solution)/shard_map/ppermute | solution.py:12
  157.6 6.5 %collective-permute-start.5 = (bf16[1,8,48,256]{3,2,1,0:T(8,128)(2,1)S(1)}, bf16[1,8,48,256]{3,2,1,0:T(8,128)(2,1)S(1)}, u32[]{:S(2)}, u32[]{:S(2)}) collective-permute-start(bf16[1,8,48,256]{3,2,1,0:T(8,128)(2,1)S(1)} %bitcast.247), channel_id=1, source_target_pairs={{0,4},{4,8},{8,12},{12,16},{16,20},{20,24},{24,28},{28,32},{32,36}... | collective-permute-start | bytes 589832 | tf_op jit(solution)/shard_map/ppermute | solution.py:12
  160.9 3.9 copy-start.4
  164.1 0.7 copy-start.2
  164.8 104.8 %collective-permute-start.7 = (bf16[3,1,48,256]{3,2,1,0:T(8,128)(2,1)}, bf16[3,1,48,256]{3,2,1,0:T(8,128)(2,1)}, u32[]{:S(2)}, u32[]{:S(2)}) collective-permute-start(bf16[3,1,48,256]{3,2,1,0:T(8,128)(2,1)} %get-tuple-element.54), channel_id=1, source_target_pairs={{1,0},{2,1},{3,2},{5,4},{6,5},{7,6},{9,8},{10,9},{11,10},{13,12},{... | collective-permute-start | bytes 221192 | tf_op jit(solution)/shard_map/ppermute | solution.py:23
  267.6 5.9 %collective-permute-start.6 = (bf16[3,1,48,256]{3,2,1,0:T(8,128)(2,1)}, bf16[3,1,48,256]{3,2,1,0:T(8,128)(2,1)S(1)}, u32[]{:S(2)}, u32[]{:S(2)}) collective-permute-start(bf16[3,1,48,256]{3,2,1,0:T(8,128)(2,1)} %get-tuple-element.53), channel_id=1, source_target_pairs={{0,1},{1,2},{2,3},{4,5},{5,6},{6,7},{8,9},{9,10},{10,11},{12,13},{... | collective-permute-start | bytes 221192 | tf_op jit(solution)/shard_map/ppermute | solution.py:20
  277.6 2.0 copy-start.5
  279.8 1.3 copy-start.3
  281.3 1.3 copy-start.1
  281.8 1.5 copy-start.7
  405.4 4.2 copy-start.8
  414.4 20.7 %all-to-all-start = ((bf16[64,1,989]{2,1,0:T(2,128)(2,1)}), bf16[64,1,989]{2,1,0:T(2,128)(2,1)S(1)}, u32[]{:S(2)}, u32[]{:S(2)}) async-start(bf16[64,1,989]{2,1,0:T(2,128)(2,1)} %convert_element_type.72), calls=%async_computation | async-start | bytes 524288 | tf_op jit(solution)/shard_map/all_to_all | solution.py:46
  422.5 19.5 %copy-start.32 = (pred[384,384]{0,1:T(8,128)(4,1)S(1)}, pred[384,384]{0,1:T(8,128)(4,1)}, u32[]{:S(2)}) copy-start(pred[384,384]{0,1:T(8,128)(4,1)} %iota_compare_fusion.2) | copy-start | bytes 442372
  436.1 18.3 %all-to-all-start.1 = ((bf16[64,1,989]{2,1,0:T(2,128)(2,1)}), bf16[64,1,989]{2,1,0:T(2,128)(2,1)S(1)}, u32[]{:S(2)}, u32[]{:S(2)}) async-start(bf16[64,1,989]{2,1,0:T(2,128)(2,1)} %copy.22), calls=%async_computation.1 | async-start | bytes 524288 | tf_op jit(solution)/shard_map/all_to_all | solution.py:148
Sparse Core Ops, SparseCore 0:
  10.8 126.5 all-gather.8
  140.9 121.3 all-gather.10
  265.9 128.8 all-gather.6
where the time goes:
time: 466 us; the launch traced here: 465 us
  waiting for transfers between devices  335 us (72%)
  starting transfers between devices  37.6 us (8%)
  matrix products  37.5 us (8%)
  local copies, waits for them, and re-layouts  26.1 us (6%)
  between operations  14.1 us (3%)
  other arithmetic  7.71 us (2%)
  blocking collectives  7.41 us (2%)
    all_gather x2, waiting for transfers between devices, causal_conv(): block_cols = lax.all_gather(weight, 'wide', axis=1, tiled=True)  200 us
    all_gather x1, waiting for transfers between devices, work_in_pieces(): blocks = [lax.all_gather(share, axis) for share in pieces]  102 us
    dot_general x54, matrix products, causal_conv(): jnp.dot(window, block_cols[kernel_tap * chan_count:(kernel_tap + 1) * cha...  18.6 us
    unnamed x71, local copies, waits for them, and re-layouts  16.3 us
    ppermute x4, starting transfers between devices, shifted(): return lax.ppermute(x, axis, pairs)  14.2 us
    all_to_all x1, waiting for transfers between devices, running(): lax.all_to_all(partial_sums.astype(jnp.bfloat16), 'wide', split_axis=0, c...  10.7 us
  transfers between devices with their start and end apart: 13, of which 11 were waited for; matrix products, arithmetic and copies ran while one was open for 10% of the time, Pallas kernels for 0%

commit v1 on v0

--- a/solution.py
+++ b/solution.py
@@ -65,7 +65,9 @@
     row_count = current.shape[1]
     col_count = current.shape[2]
     chan_count = current.shape[3]
-    block_cols = lax.all_gather(weight, "wide", axis=1, tiled=True)
+    block_cols = jnp.concatenate(
+        lax.all_to_all(jnp.stack([weight] * lax.axis_size("wide")), "wide", 0, 0), axis=1
+    )
     summed = jnp.zeros((row_count * col_count, block_cols.shape[1]), jnp.float32)
     for kernel_tap in range(27):
         time_step = kernel_tap // 9

time: 466 us -> 365 us (0.78)
  waiting for transfers between devices: 335 us -> 126 us
  local copies, waits for them, and re-layouts: 26.1 us -> 87.2 us
  starting transfers between devices: 37.6 us -> 77.7 us
    all_gather x2 -> x0, waiting for transfers between devices: 200 us -> none  [causal_conv(): block_cols = lax.all_gather(weight, 'wide', axis=1, tiled=True)]
    all_gather x1, waiting for transfers between devices: 102 us -> 0.01 us  [work_in_pieces(): blocks = [lax.all_gather(share, axis) for share in pieces]]
    ppermute x4, waiting for transfers between devices: 7.29 us -> 75.2 us  [shifted(): return lax.ppermute(x, axis, pairs)]
    slice x0 -> x58, local copies, waits for them, and re-layouts: none -> 62.8 us  [causal_conv(): block_cols[kernel_tap * chan_count:(kernel_tap + 1) * chan_count]]
    all_to_all x0 -> x2, starting transfers between devices: none -> 31.1 us  [causal_conv(): lax.all_to_all(jnp.stack([weight] * lax.axis_size('wide')), 'wide', 0, 0)]
    all_to_all x0 -> x2, waiting for transfers between devices: none -> 24.6 us  [causal_conv(): lax.all_to_all(jnp.stack([weight] * lax.axis_size('wide')), 'wide', 0, 0)]
    unnamed x71 -> x141, local copies, waits for them, and re-layouts: 16.3 us -> 8.45 us
    another operation x0 -> x2, local copies, waits for them, and re-layouts: none -> 7.16 us  [causal_conv(): jnp.stack([weight] * lax.axis_size('wide'))]
  transfers between devices with their start and end apart: 13 -> 13, of which waited for: 11 -> 6; matrix products, arithmetic and copies ran while one was open for 10% -> 29% of each run, Pallas kernels for 0% -> 0%
where the time goes in v1:
time: 365 us; the launch traced here: 362 us
  waiting for transfers between devices  126 us (35%)
  local copies, waits for them, and re-layouts  87.2 us (24%)
  starting transfers between devices  77.7 us (21%)
  matrix products  40.6 us (11%)
  between operations  14.8 us (4%)
  other arithmetic  8.46 us (2%)
  blocking collectives  7.45 us (2%)
    ppermute x4, waiting for transfers between devices, shifted(): return lax.ppermute(x, axis, pairs)  75.2 us
    slice x58, local copies, waits for them, and re-layouts, causal_conv(): block_cols[kernel_tap * chan_count:(kernel_tap + 1) * chan_count]  62.8 us
    all_to_all x2, starting transfers between devices, causal_conv(): lax.all_to_all(jnp.stack([weight] * lax.axis_size('wide')), 'wide', 0, 0)  31.1 us
    all_to_all x2, waiting for transfers between devices, causal_conv(): lax.all_to_all(jnp.stack([weight] * lax.axis_size('wide')), 'wide', 0, 0)  24.6 us
    dot_general x54, matrix products, causal_conv(): jnp.dot(window, block_cols[kernel_tap * chan_count:(kernel_tap + 1) * cha...  21.8 us
    ppermute x4, starting transfers between devices, shifted(): return lax.ppermute(x, axis, pairs)  19.5 us
    all_to_all x1, waiting for transfers between devices, running(): lax.all_to_all(partial_sums.astype(jnp.bfloat16), 'wide', split_axis=0, c...  11.7 us
    all_to_all x1, waiting for transfers between devices, moved(): lax.all_to_all(group, axis, split_axis=split_dim, concat_axis=concat_dim,...  10.6 us
  transfers between devices with their start and end apart: 13, of which 6 were waited for; matrix products, arithmetic and copies ran while one was open for 29% of the time, Pallas kernels for 0%

profile of v1, /device:TPU:8, one launch (start us, length us, event | category | flops | bytes accessed | tf_op | source)
XLA Modules:
  0.0 362.2 jit_solution(9391280591101576367)
XLA Ops:
  6.5 3.6 stack.4
  10.1 13.7 %all-to-all-start = ((bf16[64,6912,4]{1,2,0:T(4,128)(2,1)}), bf16[64,6912,4]{1,2,0:T(4,128)(2,1)S(1)}, u32[]{:S(2)}, u32[]{:S(2)}) async-start(bf16[64,6912,4]{1,2,0:T(4,128)(2,1)} %stack.4), calls=%async_computation | async-start | bytes 7077888 | tf_op jit(solution)/shard_map/all_to_all | solution.py:69
  23.8 4.2 %collective-permute-start = (bf16[1,8,48,256]{3,2,1,0:T(8,128)(2,1)}, bf16[1,8,48,256]{3,2,1,0:T(8,128)(2,1)}, u32[]{:S(2)}, u32[]{:S(2)}) collective-permute-start(bf16[1,8,48,256]{3,2,1,0:T(8,128)(2,1)} %param.5), channel_id=1, source_target_pairs={{0,8},{4,12},{8,16},{12,20},{16,24},{20,28},{24,32},{28,36},{32,40... | collective-permute-start | bytes 589832 | tf_op jit(solution)/shard_map/ppermute | solution.py:12
  28.0 5.6 %collective-permute-start.1 = (bf16[1,8,48,256]{3,2,1,0:T(8,128)(2,1)}, bf16[1,8,48,256]{3,2,1,0:T(8,128)(2,1)}, u32[]{:S(2)}, u32[]{:S(2)}) collective-permute-start(bf16[1,8,48,256]{3,2,1,0:T(8,128)(2,1)} %param.5), channel_id=1, source_target_pairs={{0,4},{4,8},{8,12},{12,16},{16,20},{20,24},{24,28},{28,32},{32,36}... | collective-permute-start | bytes 589832 | tf_op jit(solution)/shard_map/ppermute | solution.py:12
  33.6 75.2 %collective-permute-done = bf16[1,8,48,256]{3,2,1,0:T(8,128)(2,1)} collective-permute-done((bf16[1,8,48,256]{3,2,1,0:T(8,128)(2,1)}, bf16[1,8,48,256]{3,2,1,0:T(8,128)(2,1)}, u32[]{:S(2)}, u32[]{:S(2)}) %collective-permute-start) | collective-permute-done | bytes 196640 | tf_op jit(solution)/shard_map/ppermute | solution.py:12
  111.6 1.9 collective-permute-start.2
  113.5 3.6 %collective-permute-start.3 = (bf16[3,1,48,256]{3,2,1,0:T(8,128)(2,1)S(1)}, bf16[3,1,48,256]{3,2,1,0:T(8,128)(2,1)S(1)}, u32[]{:S(2)}, u32[]{:S(2)}) collective-permute-start(bf16[3,1,48,256]{3,2,1,0:T(8,128)(2,1)S(1)} %get-tuple-element.113), channel_id=1, source_target_pairs={{1,0},{2,1},{3,2},{5,4},{6,5},{7,6},{9,8},{10,9},{11,10},{13,12},{... | collective-permute-start | bytes 221192 | tf_op jit(solution)/shard_map/ppermute | solution.py:23
  120.6 1.8 fusion.84
  122.5 3.6 stack.5
  126.1 17.4 %all-to-all-start.1 = ((bf16[64,6912,4]{1,2,0:T(4,128)(2,1)}), bf16[64,6912,4]{1,2,0:T(4,128)(2,1)S(1)}, u32[]{:S(2)}, u32[]{:S(2)}) async-start(bf16[64,6912,4]{1,2,0:T(4,128)(2,1)} %stack.5), calls=%async_computation.1 | async-start | bytes 7077888 | tf_op jit(solution)/shard_map/all_to_all | solution.py:69
  143.5 2.5 fusion.82
  146.1 1.6 slice.544
  147.7 1.6 slice.547
  149.2 1.6 slice.550
  150.8 1.6 slice.553
  152.4 1.6 slice.558
  154.0 1.6 slice.555
  155.6 1.6 slice.561
  157.2 3.9 %fusion.81 = (bf16[256,64,4]{0,2,1:T(4,128)(2,1)}, bf16[256,64,4]{0,2,1:T(4,128)(2,1)}, bf16[256,64,4]{0,2,1:T(4,128)(2,1)}, bf16[256,64,4]{0,2,1:T(4,128)(2,1)}...) fusion(bf16[6912,64,4]{0,2,1:T(4,128)(2,1)} %bitcast.349), kind=kLoop, calls=%fused_computation.142 | loop fusion | bytes 4980736 | tf_op jit(solution)/shard_map/slice | solution.py:80
  161.1 1.6 slice.567
  162.7 1.6 slice.564
  164.3 1.6 slice.570
  165.9 1.6 slice.576
  167.5 1.6 slice.573
  169.1 1.6 slice.579
  170.7 1.6 slice.584
  172.3 1.6 slice.581
  173.9 1.6 slice.587
  175.5 1.6 slice.593
  177.1 1.6 slice.590
  178.7 1.6 slice.596
  180.2 1.6 slice.602
  181.8 1.6 slice.599
  183.4 1.6 slice.605
  185.0 1.6 slice.607
  186.6 1.6 slice.610
  188.2 1.6 slice.613
  189.8 1.6 slice.619
  191.4 1.6 slice.616
  193.0 1.3 fusion.87
  194.3 1.3 fusion.88
  195.6 1.3 fusion.89
  207.0 4.2 %collective-permute-start.4 = (bf16[1,8,48,256]{3,2,1,0:T(8,128)(2,1)}, bf16[1,8,48,256]{3,2,1,0:T(8,128)(2,1)}, u32[]{:S(2)}, u32[]{:S(2)}) collective-permute-start(bf16[1,8,48,256]{3,2,1,0:T(8,128)(2,1)} %bitcast.28), channel_id=1, source_target_pairs={{0,8},{4,12},{8,16},{12,20},{16,24},{20,28},{24,32},{28,36},{32,40... | collective-permute-start | bytes 589832 | tf_op jit(solution)/shard_map/ppermute | solution.py:12
  211.1 5.6 %collective-permute-start.5 = (bf16[1,8,48,256]{3,2,1,0:T(8,128)(2,1)}, bf16[1,8,48,256]{3,2,1,0:T(8,128)(2,1)}, u32[]{:S(2)}, u32[]{:S(2)}) collective-permute-start(bf16[1,8,48,256]{3,2,1,0:T(8,128)(2,1)} %bitcast.28), channel_id=1, source_target_pairs={{0,4},{4,8},{8,12},{12,16},{16,20},{20,24},{24,28},{28,32},{32,36}... | collective-permute-start | bytes 589832 | tf_op jit(solution)/shard_map/ppermute | solution.py:12
  216.7 24.6 %all-to-all-done.1 = bf16[64,6912,4]{1,2,0:T(4,128)(2,1)S(1)} async-done(((bf16[64,6912,4]{1,2,0:T(4,128)(2,1)}), bf16[64,6912,4]{1,2,0:T(4,128)(2,1)S(1)}, u32[]{:S(2)}, u32[]{:S(2)}) %all-to-all-start.1) | async-done | bytes 3538976 | tf_op jit(solution)/shard_map/all_to_all | solution.py:69
  241.3 2.1 fusion.79
  243.3 1.5 pad_maximum_fusion.18
  244.9 3.0 collective-permute-start.7
  259.5 2.0 collective-permute-start.6
  262.7 2.7 collective-permute-done.6
  266.6 1.6 select_maximum_fusion
  278.7 7.4 %all_gather.9 = bf16[384,1024]{1,0:T(8,128)(2,1)S(1)} all-gather(bf16[96,1024]{1,0:T(8,128)(2,1)S(1)} %reshape.138), channel_id=1, replica_groups=mesh['wide'=64,'narrow'=4] {'narrow'}, dimensions={0}, use_global_device_ids=true | all-gather | bytes 983040 | tf_op jit(solution)/shard_map/all_gather | solution.py:106
  286.1 5.5 %copy.31 = bf16[5,8,64,1024]{3,2,1,0:T(8,128)(2,1)S(1)} copy(bf16[5,8,64,1024]{3,1,2,0:T(8,128)(2,1)} %bitcast.350) | data formatting | bytes 10485760
  291.6 2.6 fusion.12
  295.2 1.5 convert_element_type.63
  296.7 4.2 %fusion.86 = (bf16[560]{0:T(1024)(128)(2,1)S(1)}, bf16[384,560]{0,1:T(8,128)(2,1)S(1)}) fusion(bf16[384,2240]{0,1:T(8,128)(2,1)} %convert_element_type.63, bf16[3,2240,560]{1,2,0:T(8,128)(2,1)} %param.9), kind=kOutput, calls=%fused_computation.147 | convolution fusion | flops 964668864 | bytes 4732000 | tf_op jit(solution)/shard_map/dot_general | solution.py:111
  300.9 3.2 fusion.22
  305.7 10.3 %all-to-all-start.2 = ((bf16[64,1,989]{2,1,0:T(2,128)(2,1)}), bf16[64,1,989]{2,1,0:T(2,128)(2,1)S(1)}, u32[]{:S(2)}, u32[]{:S(2)}) async-start(bf16[64,1,989]{2,1,0:T(2,128)(2,1)} %convert_element_type.72), calls=%async_computation.2 | async-start | bytes 524288 | tf_op jit(solution)/shard_map/all_to_all | solution.py:46
  316.0 3.5 fusion.49
  319.5 10.6 %all-to-all-done.2 = bf16[64,1,989]{2,1,0:T(2,128)(2,1)S(1)} async-done(((bf16[64,1,989]{2,1,0:T(2,128)(2,1)}), bf16[64,1,989]{2,1,0:T(2,128)(2,1)S(1)}, u32[]{:S(2)}, u32[]{:S(2)}) %all-to-all-start.2) | async-done | bytes 126624 | tf_op jit(solution)/shard_map/all_to_all | solution.py:46
  331.2 6.2 %all-to-all-start.3 = ((bf16[64,1,989]{2,1,0:T(2,128)(2,1)}), bf16[64,1,989]{2,1,0:T(2,128)(2,1)S(1)}, u32[]{:S(2)}, u32[]{:S(2)}) async-start(bf16[64,1,989]{2,1,0:T(2,128)(2,1)} %copy.24), calls=%async_computation.3 | async-start | bytes 524288 | tf_op jit(solution)/shard_map/all_to_all | solution.py:150
  337.5 1.8 select_reduce_fusion
  339.3 11.7 %all-to-all-done.3 = bf16[64,1,989]{2,1,0:T(2,128)(2,1)S(1)} async-done(((bf16[64,1,989]{2,1,0:T(2,128)(2,1)}), bf16[64,1,989]{2,1,0:T(2,128)(2,1)S(1)}, u32[]{:S(2)}, u32[]{:S(2)}) %all-to-all-start.3) | async-done | bytes 126624 | tf_op jit(solution)/shard_map/all_to_all | solution.py:150
  352.8 2.6 fusion.25
  (255 shorter events, 45.3 us)
Async XLA Ops:
  10.1 112.4 %all-to-all-start = ((bf16[64,6912,4]{1,2,0:T(4,128)(2,1)}), bf16[64,6912,4]{1,2,0:T(4,128)(2,1)S(1)}, u32[]{:S(2)}, u32[]{:S(2)}) async-start(bf16[64,6912,4]{1,2,0:T(4,128)(2,1)} %stack.4), calls=%async_computation | async-start | bytes 7077888 | tf_op jit(solution)/shard_map/all_to_all | solution.py:69
  23.8 262.3 %all-gather.3.cloned.1.call-start = ((), (), s32[]{:S(2)}) async-start(), calls=%async_computation.4 | async-start | bytes 5324800 | tf_op jit(solution)/shard_map/all_gather | solution.py:38
  23.8 84.9 %collective-permute-start = (bf16[1,8,48,256]{3,2,1,0:T(8,128)(2,1)}, bf16[1,8,48,256]{3,2,1,0:T(8,128)(2,1)}, u32[]{:S(2)}, u32[]{:S(2)}) collective-permute-start(bf16[1,8,48,256]{3,2,1,0:T(8,128)(2,1)} %param.5), channel_id=1, source_target_pairs={{0,8},{4,12},{8,16},{12,20},{16,24},{20,28},{24,32},{28,36},{32,40... | collective-permute-start | bytes 589832 | tf_op jit(solution)/shard_map/ppermute | solution.py:12
  28.0 81.7 %collective-permute-start.1 = (bf16[1,8,48,256]{3,2,1,0:T(8,128)(2,1)}, bf16[1,8,48,256]{3,2,1,0:T(8,128)(2,1)}, u32[]{:S(2)}, u32[]{:S(2)}) collective-permute-start(bf16[1,8,48,256]{3,2,1,0:T(8,128)(2,1)} %param.5), channel_id=1, source_target_pairs={{0,4},{4,8},{8,12},{12,16},{16,20},{20,24},{24,28},{28,32},{32,36}... | collective-permute-start | bytes 589832 | tf_op jit(solution)/shard_map/ppermute | solution.py:12
  111.6 6.3 %collective-permute-start.2 = (bf16[3,1,48,256]{3,2,1,0:T(8,128)(2,1)S(1)}, bf16[3,1,48,256]{3,2,1,0:T(8,128)(2,1)S(1)}, u32[]{:S(2)}, u32[]{:S(2)}) collective-permute-start(bf16[3,1,48,256]{3,2,1,0:T(8,128)(2,1)S(1)} %get-tuple-element.112), channel_id=1, source_target_pairs={{0,1},{1,2},{2,3},{4,5},{5,6},{6,7},{8,9},{9,10},{10,11},{12,13},{... | collective-permute-start | bytes 221192 | tf_op jit(solution)/shard_map/ppermute | solution.py:20
  113.5 5.6 %collective-permute-start.3 = (bf16[3,1,48,256]{3,2,1,0:T(8,128)(2,1)S(1)}, bf16[3,1,48,256]{3,2,1,0:T(8,128)(2,1)S(1)}, u32[]{:S(2)}, u32[]{:S(2)}) collective-permute-start(bf16[3,1,48,256]{3,2,1,0:T(8,128)(2,1)S(1)} %get-tuple-element.113), channel_id=1, source_target_pairs={{1,0},{2,1},{3,2},{5,4},{6,5},{7,6},{9,8},{10,9},{11,10},{13,12},{... | collective-permute-start | bytes 221192 | tf_op jit(solution)/shard_map/ppermute | solution.py:23
  122.5 3.6 copy-start
  126.1 115.2 %all-to-all-start.1 = ((bf16[64,6912,4]{1,2,0:T(4,128)(2,1)}), bf16[64,6912,4]{1,2,0:T(4,128)(2,1)S(1)}, u32[]{:S(2)}, u32[]{:S(2)}) async-start(bf16[64,6912,4]{1,2,0:T(4,128)(2,1)} %stack.5), calls=%async_computation.1 | async-start | bytes 7077888 | tf_op jit(solution)/shard_map/all_to_all | solution.py:69
  193.0 4.0 %copy-start.8 = (bf16[1,8,48,256]{3,2,1,0:T(8,128)(2,1)S(1)}, bf16[1,8,48,256]{3,2,1,0:T(8,128)(2,1)}, u32[]{:S(2)}) copy-start(bf16[1,8,48,256]{3,2,1,0:T(8,128)(2,1)} %get-tuple-element.86) | copy-start | bytes 589828
  193.0 4.0 %copy-start.62 = (bf16[256,256]{0,1:T(8,128)(2,1)S(1)}, bf16[256,256]{0,1:T(8,128)(2,1)}, u32[]{:S(2)}) copy-start(bf16[256,256]{0,1:T(8,128)(2,1)} %slice.576) | copy-start | bytes 393220
  193.0 4.2 %copy-start.7 = (bf16[1,8,48,256]{3,2,1,0:T(8,128)(2,1)S(1)}, bf16[1,8,48,256]{3,2,1,0:T(8,128)(2,1)}, u32[]{:S(2)}) copy-start(bf16[1,8,48,256]{3,2,1,0:T(8,128)(2,1)} %get-tuple-element.84) | copy-start | bytes 589828
  193.0 4.2 %copy-start.63 = (bf16[256,256]{0,1:T(8,128)(2,1)S(1)}, bf16[256,256]{0,1:T(8,128)(2,1)}, u32[]{:S(2)}) copy-start(bf16[256,256]{0,1:T(8,128)(2,1)} %slice.584) | copy-start | bytes 393220
  193.0 4.5 %copy-start.6 = (bf16[1,8,48,256]{3,2,1,0:T(8,128)(2,1)S(1)}, bf16[1,8,48,256]{3,2,1,0:T(8,128)(2,1)}, u32[]{:S(2)}) copy-start(bf16[1,8,48,256]{3,2,1,0:T(8,128)(2,1)} %get-tuple-element.82) | copy-start | bytes 589828
  193.0 4.5 %copy-start.64 = (bf16[256,256]{0,1:T(8,128)(2,1)S(1)}, bf16[256,256]{0,1:T(8,128)(2,1)}, u32[]{:S(2)}) copy-start(bf16[256,256]{0,1:T(8,128)(2,1)} %slice.593) | copy-start | bytes 393220
  194.3 3.4 copy-start.5
  194.3 3.4 copy-start.65
  195.6 2.4 copy-start.23
  195.6 2.4 copy-start.31
  197.2 1.1 copy-start.18
  197.2 1.1 copy-start.29
  197.5 1.1 copy-start.17
  197.5 1.1 copy-start.26
  198.3 1.9 copy-start.16
  198.3 1.9 copy-start.24
  198.6 1.9 copy-start.22
  198.6 1.9 copy-start.41
  199.0 1.8 copy-start.15
  199.0 1.8 copy-start.39
  200.5 1.0 copy-start.37
  201.2 1.8 copy-start.13
  201.2 1.8 copy-start.35
  201.6 1.8 copy-start.20
  201.6 1.8 copy-start.36
  201.8 1.8 copy-start.12
  201.8 1.8 copy-start.33
  203.4 1.0 copy-start.32
  205.0 1.0 copy-start.68
  207.0 36.3 %collective-permute-start.4 = (bf16[1,8,48,256]{3,2,1,0:T(8,128)(2,1)}, bf16[1,8,48,256]{3,2,1,0:T(8,128)(2,1)}, u32[]{:S(2)}, u32[]{:S(2)}) collective-permute-start(bf16[1,8,48,256]{3,2,1,0:T(8,128)(2,1)} %bitcast.28), channel_id=1, source_target_pairs={{0,8},{4,12},{8,16},{12,20},{16,24},{20,28},{24,32},{28,36},{32,40... | collective-permute-start | bytes 589832 | tf_op jit(solution)/shard_map/ppermute | solution.py:12
  211.1 32.2 %collective-permute-start.5 = (bf16[1,8,48,256]{3,2,1,0:T(8,128)(2,1)}, bf16[1,8,48,256]{3,2,1,0:T(8,128)(2,1)}, u32[]{:S(2)}, u32[]{:S(2)}) collective-permute-start(bf16[1,8,48,256]{3,2,1,0:T(8,128)(2,1)} %bitcast.28), channel_id=1, source_target_pairs={{0,4},{4,8},{8,12},{12,16},{16,20},{20,24},{24,28},{28,32},{32,36}... | collective-permute-start | bytes 589832 | tf_op jit(solution)/shard_map/ppermute | solution.py:12
  244.9 16.7 %collective-permute-start.7 = (bf16[3,1,48,256]{3,2,1,0:T(8,128)(2,1)}, bf16[3,1,48,256]{3,2,1,0:T(8,128)(2,1)}, u32[]{:S(2)}, u32[]{:S(2)}) collective-permute-start(bf16[3,1,48,256]{3,2,1,0:T(8,128)(2,1)} %get-tuple-element.108), channel_id=1, source_target_pairs={{1,0},{2,1},{3,2},{5,4},{6,5},{7,6},{9,8},{10,9},{11,10},{13,12},{... | collective-permute-start | bytes 221192 | tf_op jit(solution)/shard_map/ppermute | solution.py:23
  249.0 8.0 %copy-start.59 = (bf16[256,64,4]{0,2,1:T(4,128)(2,1)S(1)}, bf16[256,64,4]{0,2,1:T(4,128)(2,1)}, u32[]{:S(2)}) copy-start(bf16[256,64,4]{0,2,1:T(4,128)(2,1)} %get-tuple-element.24) | copy-start | bytes 393220
  249.0 9.0 %copy-start.58 = (bf16[256,64,4]{0,2,1:T(4,128)(2,1)S(1)}, bf16[256,64,4]{0,2,1:T(4,128)(2,1)}, u32[]{:S(2)}) copy-start(bf16[256,64,4]{0,2,1:T(4,128)(2,1)} %get-tuple-element.20) | copy-start | bytes 393220
  249.0 9.1 %copy-start.57 = (bf16[256,64,4]{0,2,1:T(4,128)(2,1)S(1)}, bf16[256,64,4]{0,2,1:T(4,128)(2,1)}, u32[]{:S(2)}) copy-start(bf16[256,64,4]{0,2,1:T(4,128)(2,1)} %get-tuple-element.21) | copy-start | bytes 393220
  249.0 9.1 %copy-start.56 = (bf16[256,64,4]{0,2,1:T(4,128)(2,1)S(1)}, bf16[256,64,4]{0,2,1:T(4,128)(2,1)}, u32[]{:S(2)}) copy-start(bf16[256,64,4]{0,2,1:T(4,128)(2,1)} %get-tuple-element.19) | copy-start | bytes 393220
  249.0 9.2 %copy-start.55 = (bf16[256,64,4]{0,2,1:T(4,128)(2,1)S(1)}, bf16[256,64,4]{0,2,1:T(4,128)(2,1)}, u32[]{:S(2)}) copy-start(bf16[256,64,4]{0,2,1:T(4,128)(2,1)} %get-tuple-element.17) | copy-start | bytes 393220
  250.1 8.8 %copy-start.54 = (bf16[256,64,4]{0,2,1:T(4,128)(2,1)S(1)}, bf16[256,64,4]{0,2,1:T(4,128)(2,1)}, u32[]{:S(2)}) copy-start(bf16[256,64,4]{0,2,1:T(4,128)(2,1)} %get-tuple-element.18) | copy-start | bytes 393220
  251.0 7.9 %copy-start.53 = (bf16[256,64,4]{0,2,1:T(4,128)(2,1)S(1)}, bf16[256,64,4]{0,2,1:T(4,128)(2,1)}, u32[]{:S(2)}) copy-start(bf16[256,64,4]{0,2,1:T(4,128)(2,1)} %get-tuple-element.16) | copy-start | bytes 393220
  252.0 7.0 %copy-start.52 = (bf16[256,64,4]{0,2,1:T(4,128)(2,1)S(1)}, bf16[256,64,4]{0,2,1:T(4,128)(2,1)}, u32[]{:S(2)}) copy-start(bf16[256,64,4]{0,2,1:T(4,128)(2,1)} %get-tuple-element.14) | copy-start | bytes 393220
  253.0 6.0 %copy-start.51 = (bf16[256,64,4]{0,2,1:T(4,128)(2,1)S(1)}, bf16[256,64,4]{0,2,1:T(4,128)(2,1)}, u32[]{:S(2)}) copy-start(bf16[256,64,4]{0,2,1:T(4,128)(2,1)} %get-tuple-element.15) | copy-start | bytes 393220
  254.0 5.1 %copy-start.50 = (bf16[256,64,4]{0,2,1:T(4,128)(2,1)S(1)}, bf16[256,64,4]{0,2,1:T(4,128)(2,1)}, u32[]{:S(2)}) copy-start(bf16[256,64,4]{0,2,1:T(4,128)(2,1)} %get-tuple-element.13) | copy-start | bytes 393220
  255.0 4.1 %copy-start.49 = (bf16[256,64,4]{0,2,1:T(4,128)(2,1)S(1)}, bf16[256,64,4]{0,2,1:T(4,128)(2,1)}, u32[]{:S(2)}) copy-start(bf16[256,64,4]{0,2,1:T(4,128)(2,1)} %get-tuple-element.11) | copy-start | bytes 393220
  256.0 3.2 copy-start.48
  257.0 2.3 copy-start.47
  257.0 2.3 copy-start.46
  258.0 1.3 copy-start.45
  258.1 1.3 copy-start.44
  258.1 1.3 copy-start.43
  258.2 1.3 copy-start.42
  259.5 5.9 %collective-permute-start.6 = (bf16[3,1,48,256]{3,2,1,0:T(8,128)(2,1)}, bf16[3,1,48,256]{3,2,1,0:T(8,128)(2,1)S(1)}, u32[]{:S(2)}, u32[]{:S(2)}) collective-permute-start(bf16[3,1,48,256]{3,2,1,0:T(8,128)(2,1)} %get-tuple-element.107), channel_id=1, source_target_pairs={{0,1},{1,2},{2,3},{4,5},{5,6},{6,7},{8,9},{9,10},{10,11},{12,13},{... | collective-permute-start | bytes 221192 | tf_op jit(solution)/shard_map/ppermute | solution.py:20
  276.3 1.7 copy-start.2
  296.7 4.2 %copy-start.3 = (bf16[384,2240]{0,1:T(8,128)(2,1)S(1)}, bf16[384,2240]{0,1:T(8,128)(2,1)}, u32[]{:S(2)}) copy-start(bf16[384,2240]{0,1:T(8,128)(2,1)} %convert_element_type.63) | copy-start | bytes 5160964
  305.7 24.5 %all-to-all-start.2 = ((bf16[64,1,989]{2,1,0:T(2,128)(2,1)}), bf16[64,1,989]{2,1,0:T(2,128)(2,1)S(1)}, u32[]{:S(2)}, u32[]{:S(2)}) async-start(bf16[64,1,989]{2,1,0:T(2,128)(2,1)} %convert_element_type.72), calls=%async_computation.2 | async-start | bytes 524288 | tf_op jit(solution)/shard_map/all_to_all | solution.py:46
  316.0 21.4 %copy-start.67 = (pred[384,384]{0,1:T(8,128)(4,1)S(1)}, pred[384,384]{0,1:T(8,128)(4,1)}, u32[]{:S(2)}) copy-start(pred[384,384]{0,1:T(8,128)(4,1)} %iota_compare_fusion.2) | copy-start | bytes 442372
  331.2 19.7 %all-to-all-start.3 = ((bf16[64,1,989]{2,1,0:T(2,128)(2,1)}), bf16[64,1,989]{2,1,0:T(2,128)(2,1)S(1)}, u32[]{:S(2)}, u32[]{:S(2)}) async-start(bf16[64,1,989]{2,1,0:T(2,128)(2,1)} %copy.24), calls=%async_computation.3 | async-start | bytes 524288 | tf_op jit(solution)/shard_map/all_to_all | solution.py:150
  (18 other events, 17.9 us)
Sparse Core Ops, SparseCore 0:
  33.7 174.2 all-gather.2
